TPU v7x, 32 devices: a whole 2x2x4 slice. The times are simulated.
32 devices in a mesh: front: 4 (over y, core), row: 8 (over z, x).
Axes of the slice: x: 2, y: 2, z: 4, core: 2. Of those that a mesh axis runs over, the one named last changes fastest.
Arguments:
- rhs_diag: float32 [4, 32, 2048], P('front', None, 'row'), may hold values from -6 to 6
- rhs_off: float32 [4, 32, 12288], P('front', None, 'row'), may hold values from -6 to 6
- diag_factor: float32 [4, 2048, 2048], P('front', 'row'), may hold values from -0.125 to 0.125
- off_factor: float32 [4, 12288, 2048], P('front', 'row'), may hold values from -0.125 to 0.125
- diag_inverse: float32 [4, 4, 512, 512], P('front')
- pattern: int32 [4, 4, 96], P('front', None, 'row'), may hold values 0 or 1
- upd_vals: float32 [32, 4, 8, 4, 8, 128], P(None, 'front', 'row'), may hold values from -4 to 4
- upd_rows: int32 [4, 8, 4, 8, 128], P('front', 'row'), may hold values from 0 to 1791
Outputs:
- solved: float32 [4, 32, 2048], P('front', None, 'row')
- remainder: float32 [4, 32, 12288], P('front', None, 'row')
Inputs may be any that keep to these rules, and one draw needn't show every extreme that they name: `upd_rows`: relative rows of the receiving row block: below 256 a window row, else a row below the window; several entries may name one row.
All inputs are finite; a program needn't handle non-finite values. No bound on the sum of `pattern` on one device may be relied on, other than what follows from the above.
Results may differ from a plain program's by a relative error of at most 0.0001.
Values sent between devices are 32-bit elements; how exact they have to be, the bound alone decides.
A program may use at most 128 MiB of HBM per device.

v0:
```python
import jax
import jax.numpy as jnp
from jax import lax
from jax.sharding import PartitionSpec as P

W = 512
P_SIZE = 4
BR = 128


def local(rhs_diag, rhs_off, diag_factor, off_factor, diag_inverse, pattern, upd_vals, upd_rows):
    own_rows = diag_factor.shape[1]
    nrhs_count = upd_vals.shape[0]
    fronts_all = upd_vals.shape[3]
    groups_all = upd_vals.shape[4]
    slot_count = upd_vals.shape[5]
    flat_vals = upd_vals.reshape(nrhs_count, 1, fronts_all * groups_all, slot_count)
    arrived = lax.all_to_all(flat_vals, ("front", "row"), split_axis=2, concat_axis=1, tiled=True)
    received = arrived.reshape(nrhs_count, -1)
    targets = upd_rows.reshape(-1)
    combined = jnp.concatenate([rhs_diag[0], rhs_off[0]], axis=1)
    combined = combined.at[:, targets].add(received)
    upper = combined[:, :own_rows]
    lower = combined[:, own_rows:]
    diag_local = diag_factor[0]
    off_local = off_factor[0]
    inverse = diag_inverse[0]
    mask_rows = jnp.repeat(pattern[0].astype(jnp.float32), BR, axis=1)
    group = lax.axis_index("row")
    positions = group * own_rows + lax.iota(jnp.int32, own_rows)
    columns = lax.iota(jnp.int32, W)
    highest = lax.Precision.HIGHEST
    contract = (((1,), (1,)), ((), ()))
    pieces = []
    for panel in range(P_SIZE):
        picker = (
            (positions[:, None] // W == panel) & (positions[:, None] % W == columns[None, :])
        ).astype(jnp.float32)
        partial_rhs = jnp.dot(upper, picker, precision=highest, preferred_element_type=jnp.float32)
        panel_rhs = lax.psum(partial_rhs, "row")
        piece = lax.dot_general(
            panel_rhs,
            inverse[panel],
            contract,
            precision=highest,
            preferred_element_type=jnp.float32,
        )
        pieces.append(piece)
        upper = upper - lax.dot_general(
            piece,
            diag_local[:, panel * W : (panel + 1) * W],
            contract,
            precision=highest,
            preferred_element_type=jnp.float32,
        )
        term = lax.dot_general(
            piece,
            off_local[:, panel * W : (panel + 1) * W],
            contract,
            precision=highest,
            preferred_element_type=jnp.float32,
        )
        lower = lower - term * mask_rows[panel][None, :]
    solution = jnp.concatenate(pieces, axis=1)
    own_solution = lax.dynamic_slice_in_dim(solution, group * own_rows, own_rows, 1)
    return (own_solution[None], lower[None])


def solution(mesh):
    in_specs = (
        P("front", None, "row"),
        P("front", None, "row"),
        P("front", "row", None),
        P("front", "row", None),
        P("front", None, None, None),
        P("front", None, "row"),
        P(None, "front", "row", None, None, None),
        P("front", "row", None, None, None),
    )
    out_specs = (P("front", None, "row"), P("front", None, "row"))
    return jax.shard_map(local, mesh=mesh, in_specs=in_specs, out_specs=out_specs, check_vma=False)
```

profile of v0, /device:TPU:0, one launch (start us, length us, event | category | flops | bytes accessed | tf_op | source)
XLA Modules:
  0.0 367.9 jit_solution(12900171675111309321)
XLA Ops:
  7.2 2.1 copy.19
  9.3 7.3 %all-to-all-start = ((f32[32,1,32,128]{3,0,1,2:T(8,128)}), f32[32,1,32,128]{3,0,1,2:T(8,128)S(1)}, u32[]{:S(2)}, u32[]{:S(2)}) async-start(f32[32,1,32,128]{3,0,1,2:T(8,128)} %bitcast.4), calls=%async_computation | async-start | bytes 1048576 | tf_op jit(solution)/shard_map/all_to_all | solution.py:18
  16.6 0.0 all-reduce.5.cloned.1.call-start
  16.7 0.5 broadcast_compare_fusion.2
  17.2 0.7 convert_element_type.3
  17.9 0.9 pad_maximum_fusion
  18.9 0.7 broadcast_bitcast_fusion
  19.5 0.7 broadcast_bitcast_fusion.2
  20.2 0.5 broadcast_compare_fusion.4
  20.7 0.3 copy.21
  21.0 0.6 and_select_fusion
  21.6 0.7 compare_select_fusion
  22.3 10.5 %all-to-all-done = f32[32,1,32,128]{3,0,1,2:T(8,128)S(1)} async-done(((f32[32,1,32,128]{3,0,1,2:T(8,128)}), f32[32,1,32,128]{3,0,1,2:T(8,128)S(1)}, u32[]{:S(2)}, u32[]{:S(2)}) %all-to-all-start) | async-done | bytes 524320 | tf_op jit(solution)/shard_map/all_to_all | solution.py:18
  32.9 0.3 copy.20
  33.2 0.3 copy.29
  33.5 0.6 copy.22
  34.1 0.0 copy-start.7
  34.1 22.7 %scatter_fusion = f32[32,1792]{0,1:T(8,128)S(1)} fusion(f32[32,1792]{0,1:T(8,128)S(1)} %copy.21, s32[4096]{0:T(1024)S(1)} %bitcast.72, f32[4096,32]{1,0:T(8,128)S(1)} %copy.22), kind=kCustom, calls=%fused_computation | custom fusion | flops 131072 | bytes 1589248 | tf_op jit(solution)/shard_map/scatter-add | solution.py:22
  56.9 1.0 fusion.54
  57.9 0.0 all-reduce.5.cloned.1.call-update
  57.9 0.0 all-reduce.7.cloned.1.call-start
  58.0 0.1 copy.25
  58.1 67.0 %all-reduce.5.cloned.1.call-done = f32[32,512]{1,0:T(8,128)} async-done(((f32[32,512]{1,0:T(8,128)}), f32[32,512]{1,0:T(8,128)}) %all-reduce.5.cloned.1.call-update) | async-done | bytes 65552 | tf_op jit(solution)/shard_map/psum | solution.py:40
  125.1 2.3 fusion.41
  127.4 1.6 convolution_subtract_fusion.2
  129.0 1.0 fusion.56
  130.0 0.0 all-reduce.7.cloned.1.call-update
  130.1 0.0 all-reduce.9.cloned.1.call-start
  130.1 0.1 slice.100
  130.2 0.2 copy.26
  130.4 69.0 %all-reduce.7.cloned.1.call-done = f32[32,512]{1,0:T(8,128)} async-done(((f32[32,512]{1,0:T(8,128)}), f32[32,512]{1,0:T(8,128)}) %all-reduce.7.cloned.1.call-update) | async-done | bytes 65552 | tf_op jit(solution)/shard_map/psum | solution.py:40
  199.4 2.3 fusion.39
  201.7 1.6 convolution_subtract_fusion.1
  203.4 1.0 fusion.58
  204.4 0.0 all-reduce.9.cloned.1.call-update
  204.4 0.2 all-reduce.11.cloned.1.call-start
  204.6 4.8 %fusion.23 = f32[32,1536]{1,0:T(8,128)S(1)} fusion(f32[32,512]{1,0:T(8,128)S(1)} %fusion.39, f32[1536,2048]{1,0:T(8,128)} %bitcast.62, f32[1536]{0:T(1024)S(1)} %copy-done.3), kind=kOutput, calls=%fused_computation.14 | convolution fusion | flops 302039040 | bytes 3414016 | tf_op jit(solution)/shard_map/dot_general | solution.py:56
  209.4 64.3 %all-reduce.9.cloned.1.call-done = f32[32,512]{1,0:T(8,128)} async-done(((f32[32,512]{1,0:T(8,128)}), f32[32,512]{1,0:T(8,128)}) %all-reduce.9.cloned.1.call-update) | async-done | bytes 65552 | tf_op jit(solution)/shard_map/psum | solution.py:40
  273.7 2.3 fusion.37
  276.1 1.6 convolution_subtract_fusion
  277.7 1.0 fusion.60
  278.7 0.0 all-reduce.11.cloned.1.call-update
  278.7 4.8 %fusion.26 = f32[32,1536]{1,0:T(8,128)S(1)} fusion(f32[32,512]{1,0:T(8,128)S(1)} %fusion.37, f32[1536,2048]{1,0:T(8,128)} %bitcast.63, f32[1536]{0:T(1024)S(1)} %copy-done.2), kind=kOutput, calls=%fused_computation.15 | convolution fusion | flops 302039040 | bytes 3414016 | tf_op jit(solution)/shard_map/dot_general | solution.py:56
  283.5 64.5 %all-reduce.11.cloned.1.call-done = f32[32,512]{1,0:T(8,128)} async-done(((f32[32,512]{1,0:T(8,128)}), f32[32,512]{1,0:T(8,128)}) %all-reduce.11.cloned.1.call-update) | async-done | bytes 65552 | tf_op jit(solution)/shard_map/psum | solution.py:40
  348.1 2.3 fusion.35
  350.4 4.8 %fusion.29 = f32[32,1536]{1,0:T(8,128)S(1)} fusion(f32[32,512]{1,0:T(8,128)S(1)} %fusion.35, f32[1536,2048]{1,0:T(8,128)} %bitcast.64, f32[1536]{0:T(1024)S(1)} %copy-done.1), kind=kOutput, calls=%fused_computation.16 | convolution fusion | flops 302039040 | bytes 3414016 | tf_op jit(solution)/shard_map/dot_general | solution.py:56
  355.2 0.6 fusion.73
  355.8 5.5 %fusion.32 = f32[1,32,1536]{2,1,0:T(8,128)} fusion(f32[32,1536]{1,0:T(8,128)S(1)} %fusion.29, f32[32,1536]{1,0:T(8,128)S(1)} %fusion.26, f32[32,1536]{1,0:T(8,128)S(1)} %fusion.23, f32[32,1536]{1,0:T(8,128)S(1)} %copy.26, f32[32,512]{1,0:T(8,128)S(1)} %fusion.41, f32[1536,2048]{1,0:T(8,128)} %bitcast.65, f32[1536]{0:T(1024)S(1)} %copy-done), kind=kOutput, calls=%fused_computation.17 | convolution fusion | flops 302235648 | bytes 4200448 | tf_op jit(solution)/shard_map/dot_general | solution.py:56
  (19 shorter events, 0.1 us)
Async XLA Ops:
  9.3 23.6 %all-to-all-start = ((f32[32,1,32,128]{3,0,1,2:T(8,128)}), f32[32,1,32,128]{3,0,1,2:T(8,128)S(1)}, u32[]{:S(2)}, u32[]{:S(2)}) async-start(f32[32,1,32,128]{3,0,1,2:T(8,128)} %bitcast.4), calls=%async_computation | async-start | bytes 1048576 | tf_op jit(solution)/shard_map/all_to_all | solution.py:18
  16.6 108.5 %all-reduce.5.cloned.1.call-start = ((), (), s32[]{:S(2)}) async-start(), calls=%async_computation.1 | async-start | bytes 131072 | tf_op jit(solution)/shard_map/psum | solution.py:40
  34.1 22.8 %copy-start.4 = (s32[256]{0:T(256)S(1)}, s32[256]{0:T(256)}, u32[]{:S(2)}) copy-start(s32[256]{0:T(256)} %and_select_fusion) | copy-start | bytes 3076
  34.1 22.8 %copy-start.7 = (pred[256]{0:T(512)(128)(4,1)S(1)}, pred[256]{0:T(512)(128)(4,1)}, u32[]{:S(2)}) copy-start(pred[256]{0:T(512)(128)(4,1)} %broadcast_compare_fusion.2) | copy-start | bytes 772
  34.1 94.9 %copy-start.6 = (pred[256]{0:T(512)(128)(4,1)S(1)}, pred[256]{0:T(512)(128)(4,1)}, u32[]{:S(2)}) copy-start(pred[256]{0:T(512)(128)(4,1)} %broadcast_compare_fusion.4) | copy-start | bytes 772
  56.9 146.5 %copy-start.5 = (s32[256]{0:T(256)S(1)}, s32[256]{0:T(256)}, u32[]{:S(2)}) copy-start(s32[256]{0:T(256)} %and_select_fusion) | copy-start | bytes 3076
  56.9 147.7 %copy-start.3 = (f32[1536]{0:T(1024)S(1)}, f32[1536]{0:T(1024)}, u32[]{:S(2)}) copy-start(f32[1536]{0:T(1024)} %get-tuple-element.8) | copy-start | bytes 18436
  57.9 141.5 %all-reduce.7.cloned.1.call-start = ((), (), s32[]{:S(2)}) async-start(), calls=%async_computation.2 | async-start | bytes 131072 | tf_op jit(solution)/shard_map/psum | solution.py:40
  130.1 143.7 %all-reduce.9.cloned.1.call-start = ((), (), s32[]{:S(2)}) async-start(), calls=%async_computation.3 | async-start | bytes 131072 | tf_op jit(solution)/shard_map/psum | solution.py:40
  130.2 148.5 %copy-start.2 = (f32[1536]{0:T(1024)S(1)}, f32[1536]{0:T(1024)}, u32[]{:S(2)}) copy-start(f32[1536]{0:T(1024)} %get-tuple-element.7) | copy-start | bytes 18436
  204.4 143.7 %all-reduce.11.cloned.1.call-start = ((), (), s32[]{:S(2)}) async-start(), calls=%async_computation.4 | async-start | bytes 131072 | tf_op jit(solution)/shard_map/psum | solution.py:40
  209.4 140.9 %copy-start.1 = (f32[1536]{0:T(1024)S(1)}, f32[1536]{0:T(1024)}, u32[]{:S(2)}) copy-start(f32[1536]{0:T(1024)} %get-tuple-element.6) | copy-start | bytes 18436
  278.7 77.2 %copy-start = (f32[1536]{0:T(1024)S(1)}, f32[1536]{0:T(1024)}, u32[]{:S(2)}) copy-start(f32[1536]{0:T(1024)} %get-tuple-element.9) | copy-start | bytes 18436
Sparse Core Ops, SparseCore 0:
  58.0 66.9 all-reduce.4
  130.2 69.1 all-reduce.6
  204.5 69.1 all-reduce.8
  278.8 69.1 all-reduce.10
where the time goes:
time: 369 us; the launch traced here: 368 us
  waiting for transfers between devices  275 us (75%)
  matrix products  37.9 us (10%)
  other arithmetic  27.4 us (7%)
  between operations  14 us (4%)
  starting transfers between devices  7.67 us (2%)
  local copies, waits for them, and re-layouts  5.4 us (1%)
    psum x4, waiting for transfers between devices, local(): panel_rhs = lax.psum(partial_rhs, 'row')  265 us
    scatter-add x1, other arithmetic, local(): combined = combined.at[:, targets].add(received)  22.7 us
    dot_general x4, matrix products, local(): lax.dot_general(piece, off_local[:, panel * W:(panel + 1) * W], contract,...  19.9 us
    all_to_all x1, waiting for transfers between devices, local(): lax.all_to_all(flat_vals, ('front', 'row'), split_axis=2, concat_axis=1,...  10.5 us
    dot_general x4, matrix products, local(): lax.dot_general(panel_rhs, inverse[panel], contract, precision=highest, p...  9.18 us
  transfers between devices with their start and end apart: 5, of which 5 were waited for; matrix products, arithmetic and copies ran while one was open for 4% of the time, Pallas kernels for 0%

commit v1 on v0

v1 whole, which is shorter than its diff:
```python
import functools

import jax
import jax.numpy as jnp
from jax import lax
from jax.experimental import pallas as pl
from jax.experimental.pallas import tpu as pltpu
from jax.sharding import PartitionSpec as P

W = 512
BR = 128
MESH = pl.DeviceIdType.MESH
NT = (((1,), (1,)), ((), ()))


def split(x):
    hi = x.astype(jnp.bfloat16)
    lo = (x - hi.astype(jnp.float32)).astype(jnp.bfloat16)
    return hi, lo


def dot_nt(a, b):
    return lax.dot_general(a, b, NT, preferred_element_type=jnp.float32)


def dot3(a2, b_hi, b_lo):
    n = a2.shape[0] // 2
    top = dot_nt(a2, b_hi)
    return top[:n] + top[n:] + dot_nt(a2[:n], b_lo)


def kernel(nf, nr, rd_ref, ro_ref, diag_hbm, off_hbm, inv_hbm, pat_ref, vals_hbm, rows_ref,
           solved_ref, rem_ref,
           diag_f, off_f, inv_f, diag_h, diag_l, off_h, off_l, inv_h, inv_l,
           recv, vs, upper, rhsbuf, load_sem, own_sem, a2a_send, a2a_recv, pan_send, pan_recv):
    f = lax.axis_index("front")
    r = lax.axis_index("row")
    devices = nf * nr
    nrhs, rd = upper.shape
    od = off_f.shape[0]
    panels = inv_f.shape[0]
    per = W // rd
    slot = recv.shape[3]

    load_inv = pltpu.make_async_copy(inv_hbm.at[0], inv_f, load_sem.at[0])
    load_diag = pltpu.make_async_copy(diag_hbm.at[0], diag_f, load_sem.at[1])
    load_off = pltpu.make_async_copy(off_hbm.at[0], off_f, load_sem.at[2])

    def peer(d):
        return lax.rem(f + d // nr, nf), lax.rem(r + lax.rem(d, nr), nr)

    barrier = pltpu.get_barrier_semaphore()

    def greet(d, c):
        pf, pr = peer(d)
        pl.semaphore_signal(barrier, inc=1, device_id=(pf, pr), device_id_type=MESH)
        return c

    lax.fori_loop(1, devices, greet, 0)
    load_inv.start()
    load_diag.start()
    load_off.start()
    own = pltpu.make_async_copy(vals_hbm.at[f, r], recv.at[f, r], own_sem)
    own.start()
    pl.semaphore_wait(barrier, devices - 1)

    def exchange(d):
        pf, pr = peer(d)
        return pltpu.make_async_remote_copy(
            src_ref=vals_hbm.at[pf, pr],
            dst_ref=recv.at[f, r],
            send_sem=a2a_send.at[d],
            recv_sem=a2a_recv.at[d],
            device_id=(pf, pr),
            device_id_type=MESH,
        )

    def send(d, c):
        exchange(d).start()
        return c

    lax.fori_loop(1, devices, send, 0)

    load_inv.wait()
    for p in range(panels):
        def split_inv(i, c, p=p):
            at = pl.ds(pl.multiple_of(i * 64, 64), 64)
            hi, lo = split(inv_f[p, at, :])
            inv_h[p, at, :] = hi
            inv_l[p, at, :] = lo
            return c

        lax.fori_loop(0, W // 64, split_inv, 0)
    load_diag.wait()

    def split_diag(i, c):
        at = pl.ds(pl.multiple_of(i * 16, 16), 16)
        hi, lo = split(diag_f[at, :])
        diag_h[at, :] = hi
        diag_l[at, :] = lo
        return c

    lax.fori_loop(0, rd // 16, split_diag, 0)
    load_off.wait()

    def split_off(i, c):
        at = pl.ds(pl.multiple_of(i * 16, 16), 16)
        hi, lo = split(off_f[at, :])
        off_h[at, :] = hi
        off_l[at, :] = lo
        return c

    lax.fori_loop(0, od // 16, split_off, 0)

    own.wait()

    def arrive(d, c):
        exchange(d).wait_recv()
        return c

    lax.fori_loop(1, devices, arrive, 0)

    for sf in range(nf):
        def split_vals(sr, c, sf=sf):
            hi, lo = split(recv[sf, sr])
            at = pl.ds(pl.multiple_of((sf * nr + sr) * slot, slot), slot)
            vs[pl.ds(0, nrhs), at] = hi
            vs[pl.ds(nrhs, nrhs), at] = lo
            return c

        lax.fori_loop(0, nr, split_vals, 0)

    group = 4

    def scatter(first, count):
        ids = first + lax.broadcasted_iota(jnp.int32, (count, slot), 0)

        def step(k, acc):
            rows = rows_ref[pl.ds(k * group, group), :]
            hot = jnp.concatenate(
                [jnp.where(rows[g:g + 1, :] == ids, 1.0, 0.0).astype(jnp.bfloat16) for g in range(group)], axis=1)
            at = pl.ds(pl.multiple_of(k * group * slot, group * slot), group * slot)
            return acc + dot_nt(vs[:, at], hot)

        acc = lax.fori_loop(0, devices // group, step, jnp.zeros((2 * nrhs, count), jnp.float32))
        return acc[:nrhs] + acc[nrhs:]

    upper[...] = rd_ref[0] + scatter(0, rd)

    chunk = 2 * BR
    chunks = od // chunk

    def scatter_lower(i, c):
        base = pl.multiple_of(i * chunk, chunk)
        at = pl.ds(base, chunk)
        rem_ref[0, :, at] = ro_ref[0, :, at] + scatter(rd + base, chunk)
        return c

    def off_update(p, piece2):
        def step(i, c):
            at = pl.ds(pl.multiple_of(i * chunk, chunk), chunk)
            columns = pl.ds(p * W, W)
            term = dot3(piece2, off_h[at, columns], off_l[at, columns])
            scaled = jnp.concatenate(
                [term[:, b * BR:(b + 1) * BR] * pat_ref[0, p, 2 * i + b].astype(jnp.float32) for b in range(2)], axis=1)
            rem_ref[0, :, at] -= scaled
            return c

        lax.fori_loop(0, chunks, step, 0)

    def share(d):
        return pltpu.make_async_remote_copy(
            src_ref=rhsbuf.at[r],
            dst_ref=rhsbuf.at[r],
            send_sem=pan_send.at[d],
            recv_sem=pan_recv.at[r],
            device_id=(f, lax.rem(r + d, nr)),
            device_id_type=MESH,
        )

    piece2 = None
    for p in range(panels):
        @pl.when(r // per == p)
        def _():
            rhsbuf[r] = upper[...]

            def start(d, c):
                share(d).start()
                return c

            lax.fori_loop(1, nr, start, 0)

        if p == 0:
            lax.fori_loop(0, chunks, scatter_lower, 0)
        else:
            off_update(p - 1, piece2)

        for j in range(p * per, (p + 1) * per):
            @pl.when(r != j)
            def _(j=j):
                pltpu.make_async_remote_copy(
                    src_ref=rhsbuf.at[j],
                    dst_ref=rhsbuf.at[j],
                    send_sem=pan_send.at[0],
                    recv_sem=pan_recv.at[j],
                    device_id=(f, j),
                    device_id_type=MESH,
                ).wait_recv()

        panel_rhs = jnp.concatenate([rhsbuf[j] for j in range(p * per, (p + 1) * per)], axis=1)
        piece = dot3(jnp.concatenate(split(panel_rhs), axis=0), inv_h[p], inv_l[p])
        piece2 = jnp.concatenate(split(piece), axis=0)
        if p < panels - 1:
            @pl.when(r // per > p)
            def _(piece2=piece2, p=p):
                columns = pl.ds(p * W, W)
                upper[...] -= dot3(piece2, diag_h[:, columns], diag_l[:, columns])

        for i in range(per):
            @pl.when(r == p * per + i)
            def _(i=i, piece=piece):
                solved_ref[0] = piece[:, i * rd:(i + 1) * rd]

    off_update(panels - 1, piece2)

    def sent(d, c):
        exchange(d).wait_send()
        return c

    lax.fori_loop(1, devices, sent, 0)

    def shared(d, c):
        share(d).wait_send()
        return c

    lax.fori_loop(1, nr, shared, 0)


def local(nf, nr, rhs_diag, rhs_off, diag_factor, off_factor, diag_inverse, pattern, upd_vals, upd_rows):
    nrhs = upd_vals.shape[0]
    slot = upd_vals.shape[5]
    rd = diag_factor.shape[1]
    od = off_factor.shape[1]
    k = diag_factor.shape[2]
    panels = diag_inverse.shape[1]
    devices = nf * nr
    vals = jnp.transpose(upd_vals[:, 0, 0], (1, 2, 0, 3))
    rows = upd_rows.reshape(devices, slot)
    vmem = pl.BlockSpec(memory_space=pltpu.VMEM)
    anywhere = pl.BlockSpec(memory_space=pl.ANY)
    f32, bf16 = jnp.float32, jnp.bfloat16
    return pl.pallas_call(
        functools.partial(kernel, nf, nr),
        out_shape=(
            jax.ShapeDtypeStruct((1, nrhs, rd), f32),
            jax.ShapeDtypeStruct((1, nrhs, od), f32),
        ),
        in_specs=[vmem, vmem, anywhere, anywhere, anywhere,
                  pl.BlockSpec(memory_space=pltpu.SMEM), anywhere, vmem],
        out_specs=(vmem, vmem),
        scratch_shapes=[
            pltpu.VMEM((rd, k), f32),
            pltpu.VMEM((od, k), f32),
            pltpu.VMEM((panels, W, W), f32),
            pltpu.VMEM((rd, k), bf16),
            pltpu.VMEM((rd, k), bf16),
            pltpu.VMEM((od, k), bf16),
            pltpu.VMEM((od, k), bf16),
            pltpu.VMEM((panels, W, W), bf16),
            pltpu.VMEM((panels, W, W), bf16),
            pltpu.VMEM((nf, nr, nrhs, slot), f32),
            pltpu.VMEM((2 * nrhs, devices * slot), bf16),
            pltpu.VMEM((nrhs, rd), f32),
            pltpu.VMEM((nr, nrhs, rd), f32),
            pltpu.SemaphoreType.DMA((3,)),
            pltpu.SemaphoreType.DMA,
            pltpu.SemaphoreType.DMA((devices,)),
            pltpu.SemaphoreType.DMA((devices,)),
            pltpu.SemaphoreType.DMA((nr,)),
            pltpu.SemaphoreType.DMA((nr,)),
        ],
        compiler_params=pltpu.CompilerParams(
            collective_id=0, has_side_effects=True, vmem_limit_bytes=58 * 1024 * 1024),
    )(rhs_diag, rhs_off, diag_factor, off_factor, diag_inverse, pattern, vals, rows)


def solution(mesh):
    in_specs = (
        P("front", None, "row"),
        P("front", None, "row"),
        P("front", "row", None),
        P("front", "row", None),
        P("front", None, None, None),
        P("front", None, "row"),
        P(None, "front", "row", None, None, None),
        P("front", "row", None, None, None),
    )
    out_specs = (P("front", None, "row"), P("front", None, "row"))
    body = functools.partial(local, mesh.shape["front"], mesh.shape["row"])
    return jax.shard_map(body, mesh=mesh, in_specs=in_specs, out_specs=out_specs, check_vma=False)
```

time: 369 us -> 57.1 us (0.15)
  waiting for transfers between devices: 275 us -> 0 us
  Pallas kernels: 0 us -> 51 us
  matrix products: 37.9 us -> 0 us
  other arithmetic: 27.4 us -> 0 us
  between operations: 14 us -> 0.64 us
  starting transfers between devices: 7.67 us -> 0 us
    psum x4 -> x0, waiting for transfers between devices: 265 us -> none  [local(): panel_rhs = lax.psum(partial_rhs, 'row')]
    pallas_call x0 -> x1, Pallas kernels: none -> 51 us  [local(): pl.pallas_call(functools.partial(kernel, nf, nr), out_shape=(jax.ShapeDty...]
    dot_general x15 -> x0, matrix products: 37.9 us -> none  [the longest x4 19.9 us: local(): lax.dot_general(piece, off_local[:, panel * W:(panel + 1) * W], contract,...]
    scatter-add x1 -> x0, other arithmetic: 22.7 us -> none  [local(): combined = combined.at[:, targets].add(received)]
    all_to_all x1 -> x0, waiting for transfers between devices: 10.5 us -> none  [local(): lax.all_to_all(flat_vals, ('front', 'row'), split_axis=2, concat_axis=1,...]
    all_to_all x1 -> x0, starting transfers between devices: 7.33 us -> none  [local(): lax.all_to_all(flat_vals, ('front', 'row'), split_axis=2, concat_axis=1,...]
  transfers between devices with their start and end apart: 5 -> 0, of which waited for: 5 -> 0; matrix products, arithmetic and copies ran while one was open for 4% -> 0% of each run, Pallas kernels for 0% -> 0%
where the time goes in v1:
time: 57.1 us; the launch traced here: 56.8 us
  Pallas kernels  51 us (89%)
  local copies, waits for them, and re-layouts  5.12 us (9%)
  between operations  0.64 us (1%)
    pallas_call x1, Pallas kernels, local(): pl.pallas_call(functools.partial(kernel, nf, nr), out_shape=(jax.ShapeDty...  51 us
    unnamed x3, local copies, waits for them, and re-layouts  5.12 us

profile of v1, /device:TPU:0, one launch (start us, length us, event | category | flops | bytes accessed | tf_op | source)
XLA Modules:
  0.0 56.8 jit_solution(441660492992819087)
XLA Ops:
  0.6 2.1 %copy.12 = f32[32,1,1,4,8,128]{5,0,4,3,2,1:T(8,128)} copy(f32[32,1,1,4,8,128]{5,4,3,2,1,0:T(8,128)} %param.14) | data formatting | bytes 1048576 | tf_op args[6]
  2.8 51.0 %shard_map.95 = (f32[1,32,256]{2,1,0:T(8,128)}, f32[1,32,1536]{2,1,0:T(8,128)}) custom-call(f32[1,32,256]{2,1,0:T(8,128)} %rd_ref.1, f32[1,32,1536]{2,1,0:T(8,128)} %ro_ref.1, f32[1,256,2048]{2,1,0:T(8,128)} %diag_hbm.1, f32[1,1536,2048]{2,1,0:T(8,128)} %off_hbm.1, f32[1,4,512,512]{3,2,1,0:T(8,128)} %inv_hbm.1, s32[1,4,12]{2,1,0:T(4,128)} %pat_ref.1, ...), custom_call_target="tpu_custom_call" | custom-call | tf_op jit(solution)/shard_map/pallas_call | solution.py:252
  53.8 1.4 %copy.15 = f32[1,32,256]{2,1,0:T(8,128)} copy(f32[1,32,256]{2,1,0:T(8,128)} %get-tuple-element.4) | data formatting | bytes 65536
  55.2 1.6 %copy.16 = f32[1,32,1536]{2,1,0:T(8,128)} copy(f32[1,32,1536]{2,1,0:T(8,128)} %get-tuple-element.5) | data formatting | bytes 393216

commit v2 on v1

--- a/solution.py
+++ b/solution.py
@@ -10,6 +10,7 @@
 W = 512
 BR = 128
 MESH = pl.DeviceIdType.MESH
+PART = 256
 NT = (((1,), (1,)), ((), ()))
 
 
@@ -32,7 +33,7 @@
 def kernel(nf, nr, rd_ref, ro_ref, diag_hbm, off_hbm, inv_hbm, pat_ref, vals_hbm, rows_ref,
            solved_ref, rem_ref,
            diag_f, off_f, inv_f, diag_h, diag_l, off_h, off_l, inv_h, inv_l,
-           recv, vs, upper, rhsbuf, load_sem, own_sem, a2a_send, a2a_recv, pan_send, pan_recv):
+           recv, vs, hot, code_ref, low_acc, upper, rhsbuf, load_sem, own_sem, a2a_send, a2a_recv, pan_send, pan_recv):
     f = lax.axis_index("front")
     r = lax.axis_index("row")
     devices = nf * nr
@@ -60,14 +61,14 @@
     load_inv.start()
     load_diag.start()
     load_off.start()
-    own = pltpu.make_async_copy(vals_hbm.at[f, r], recv.at[f, r], own_sem)
+    own = pltpu.make_async_copy(vals_hbm.at[:, f, r, :], recv.at[f, r], own_sem)
     own.start()
     pl.semaphore_wait(barrier, devices - 1)
 
     def exchange(d):
         pf, pr = peer(d)
         return pltpu.make_async_remote_copy(
-            src_ref=vals_hbm.at[pf, pr],
+            src_ref=vals_hbm.at[:, pf, pr, :],
             dst_ref=recv.at[f, r],
             send_sem=a2a_send.at[d],
             recv_sem=a2a_recv.at[d],
@@ -80,6 +81,17 @@
         return c
 
     lax.fori_loop(1, devices, send, 0)
+
+    code_ref[...] = rows_ref[...] + (PART - rd)
+
+    def mark(s, c):
+        low = code_ref[pl.ds(s, 1), :] & (PART - 1)
+        ids = lax.broadcasted_iota(jnp.int32, (PART, slot), 0)
+        at = pl.ds(pl.multiple_of(s * slot, slot), slot)
+        hot[:, at] = jnp.where(low == ids, 1.0, 0.0).astype(jnp.bfloat16)
+        return c
+
+    lax.fori_loop(0, devices, mark, 0)
 
     load_inv.wait()
     for p in range(panels):
@@ -131,30 +143,48 @@
         lax.fori_loop(0, nr, split_vals, 0)
 
     group = 4
-
-    def scatter(first, count):
-        ids = first + lax.broadcasted_iota(jnp.int32, (count, slot), 0)
-
-        def step(k, acc):
-            rows = rows_ref[pl.ds(k * group, group), :]
-            hot = jnp.concatenate(
-                [jnp.where(rows[g:g + 1, :] == ids, 1.0, 0.0).astype(jnp.bfloat16) for g in range(group)], axis=1)
-            at = pl.ds(pl.multiple_of(k * group * slot, group * slot), group * slot)
-            return acc + dot_nt(vs[:, at], hot)
-
-        acc = lax.fori_loop(0, devices // group, step, jnp.zeros((2 * nrhs, count), jnp.float32))
-        return acc[:nrhs] + acc[nrhs:]
-
-    upper[...] = rd_ref[0] + scatter(0, rd)
+    span = group * slot
+
+    def picked(k, parts):
+        block = code_ref[pl.ds(k * group, group), :]
+        part = jnp.concatenate([block[g:g + 1, :] for g in range(group)], axis=1) >> 8
+        values = vs[:, pl.ds(pl.multiple_of(k * span, span), span)]
+        rows = []
+        for h in parts:
+            mask = jnp.where(jnp.broadcast_to(part, (16, span)) == h, 1.0, 0.0).astype(jnp.bfloat16)
+            rows.append(values * jnp.concatenate([mask] * (2 * nrhs // 16), axis=0))
+        return jnp.concatenate(rows, axis=0)
+
+    def reduced(acc, h):
+        return acc[2 * h * nrhs:(2 * h + 1) * nrhs] + acc[(2 * h + 1) * nrhs:(2 * h + 2) * nrhs]
+
+    steps = devices // group
+    unroll = 8
+
+    def upper_step(i, acc):
+        for u in range(unroll):
+            k = i * unroll + u
+            acc = acc + dot_nt(picked(k, [0]), hot[:, pl.ds(pl.multiple_of(k * span, span), span)])
+        return acc
+
+    acc = lax.fori_loop(0, steps // unroll, upper_step, jnp.zeros((2 * nrhs, PART), jnp.float32))
+    upper[...] = rd_ref[0] + reduced(acc, 0)[:, PART - rd:]
 
     chunk = 2 * BR
     chunks = od // chunk
-
-    def scatter_lower(i, c):
-        base = pl.multiple_of(i * chunk, chunk)
-        at = pl.ds(base, chunk)
-        rem_ref[0, :, at] = ro_ref[0, :, at] + scatter(rd + base, chunk)
-        return c
+    parts = list(range(1, chunks + 1))
+
+    def scatter_lower():
+        low_acc[...] = jnp.zeros_like(low_acc)
+
+        def step(k, c):
+            low_acc[...] += dot_nt(picked(k, parts), hot[:, pl.ds(pl.multiple_of(k * span, span), span)])
+            return c
+
+        lax.fori_loop(0, steps, step, 0)
+        for h in range(chunks):
+            at = pl.ds(h * chunk, chunk)
+            rem_ref[0, :, at] = ro_ref[0, :, at] + reduced(low_acc, h)
 
     def off_update(p, piece2):
         def step(i, c):
@@ -191,7 +221,7 @@
             lax.fori_loop(1, nr, start, 0)
 
         if p == 0:
-            lax.fori_loop(0, chunks, scatter_lower, 0)
+            scatter_lower()
         else:
             off_update(p - 1, piece2)
 
@@ -244,7 +274,7 @@
     k = diag_factor.shape[2]
     panels = diag_inverse.shape[1]
     devices = nf * nr
-    vals = jnp.transpose(upd_vals[:, 0, 0], (1, 2, 0, 3))
+    vals = upd_vals.reshape(upd_vals.shape[0], nf, nr, slot)
     rows = upd_rows.reshape(devices, slot)
     vmem = pl.BlockSpec(memory_space=pltpu.VMEM)
     anywhere = pl.BlockSpec(memory_space=pl.ANY)
@@ -270,6 +300,9 @@
             pltpu.VMEM((panels, W, W), bf16),
             pltpu.VMEM((nf, nr, nrhs, slot), f32),
             pltpu.VMEM((2 * nrhs, devices * slot), bf16),
+            pltpu.VMEM((PART, devices * slot), bf16),
+            pltpu.VMEM((devices, slot), jnp.int32),
+            pltpu.VMEM((2 * nrhs * od // PART, PART), f32),
             pltpu.VMEM((nrhs, rd), f32),
             pltpu.VMEM((nr, nrhs, rd), f32),
             pltpu.SemaphoreType.DMA((3,)),

time: 57.1 us -> 47.8 us (0.84)
  Pallas kernels: 51 us -> 43.9 us
  local copies, waits for them, and re-layouts: 5.12 us -> 2.99 us
    pallas_call x1, Pallas kernels: 51 us -> 43.9 us  [local(): pl.pallas_call(functools.partial(kernel, nf, nr), out_shape=(jax.ShapeDty...]
    unnamed x3 -> x2, local copies, waits for them, and re-layouts: 5.12 us -> 2.99 us
where the time goes in v2:
time: 47.8 us; the launch traced here: 47.5 us
  Pallas kernels  43.9 us (92%)
  local copies, waits for them, and re-layouts  2.99 us (6%)
  between operations  0.64 us (1%)
    pallas_call x1, Pallas kernels, local(): pl.pallas_call(functools.partial(kernel, nf, nr), out_shape=(jax.ShapeDty...  43.9 us
    unnamed x2, local copies, waits for them, and re-layouts  2.99 us

profile of v2, /device:TPU:0, one launch (start us, length us, event | category | flops | bytes accessed | tf_op | source)
XLA Modules:
  0.0 47.5 jit_solution(6204753464475210070)
XLA Ops:
  0.6 43.9 %shard_map.95 = (f32[1,32,256]{2,1,0:T(8,128)}, f32[1,32,1536]{2,1,0:T(8,128)}) custom-call(f32[1,32,256]{2,1,0:T(8,128)} %rd_ref.1, f32[1,32,1536]{2,1,0:T(8,128)} %ro_ref.1, f32[1,256,2048]{2,1,0:T(8,128)} %diag_hbm.1, f32[1,1536,2048]{2,1,0:T(8,128)} %off_hbm.1, f32[1,4,512,512]{3,2,1,0:T(8,128)} %inv_hbm.1, s32[1,4,12]{2,1,0:T(4,128)} %pat_ref.1, ...), custom_call_target="tpu_custom_call" | custom-call | tf_op jit(solution)/shard_map/pallas_call | solution.py:282
  44.5 1.4 %copy.12 = f32[1,32,256]{2,1,0:T(8,128)} copy(f32[1,32,256]{2,1,0:T(8,128)} %get-tuple-element.4) | data formatting | bytes 65536
  45.9 1.6 %copy.13 = f32[1,32,1536]{2,1,0:T(8,128)} copy(f32[1,32,1536]{2,1,0:T(8,128)} %get-tuple-element.5) | data formatting | bytes 393216
